TPU v7x, 512 devices: a whole 4x8x8 slice. The times are simulated.
512 devices in a mesh: vert: 64 (over x, y, core), frame: 8 (over z).
Axes of the slice: x: 4, y: 8, z: 8, core: 2. Of those that a mesh axis runs over, the one named last changes fastest.
Arguments:
- animated: float32 [1024, 3, 131072], P('frame', None, 'vert'), may hold values from -10 to 10
- rest_positions: float32 [3, 131072], P(None, 'vert'), may hold values from -4 to 4
- labels: int32 [131072], P('vert'), may hold values from 0 to 63
- weight_prior: float32 [64, 131072], P(None, 'vert'), may hold values from 0.002 to 0.12
Outputs:
- new_weights: float32 [64, 131072], P(None, 'vert')
- fit_error: float32 [], replicated
All inputs are finite; a program needn't handle non-finite values.
Results may differ from a plain program's by a relative error of at most 0.0005.
Values sent between devices are 32-bit elements; how exact they have to be, the bound alone decides.
A program may use at most 64 MiB of HBM per device.

v0:
```python
import jax
import jax.numpy as jnp
from jax import lax
from jax.sharding import PartitionSpec as P

ridge_scale = 0.0001
step_size = 0.005


def bone_features(weights, homogeneous):
    return (weights[:, None, :] * homogeneous[None, :, :]).reshape(
        4 * weights.shape[0], weights.shape[1]
    )


def start_weights(labels, weight_prior):
    bones = weight_prior.shape[0]
    onehot = (labels[None, :] == jnp.arange(bones, dtype=jnp.int32)[:, None]).astype(jnp.float32)
    summed = onehot + weight_prior
    return summed / jnp.sum(summed, axis=0, keepdims=True)


def solve_normal(factor, right_sides):
    middle = lax.linalg.triangular_solve(factor, right_sides.T, left_side=True, lower=True)
    return lax.linalg.triangular_solve(factor, middle, left_side=True, lower=True, transpose_a=True)


def local(animated, rest_positions, labels, weight_prior):
    highest = lax.Precision.HIGHEST
    bones, local_verts = weight_prior.shape
    joint = 4 * bones
    verts_total = local_verts * lax.axis_size("vert")
    frames_total = animated.shape[0] * lax.axis_size("frame")
    homogeneous = jnp.concatenate([rest_positions, jnp.ones((1, local_verts), jnp.float32)], 0)
    weights = start_weights(labels, weight_prior)
    features = bone_features(weights, homogeneous)
    frame_rows = animated.reshape(-1, local_verts)
    gram_part = lax.dot_general(features, features, (((1,), (1,)), ((), ())), precision=highest)
    rhs_part = lax.dot_general(frame_rows, features, (((1,), (1,)), ((), ())), precision=highest)
    ridge = ridge_scale * verts_total * jnp.eye(joint, dtype=jnp.float32)
    gram_matrix, right_sides = lax.psum((gram_part, rhs_part), "vert")
    factor = jnp.linalg.cholesky(gram_matrix + ridge)
    transforms = solve_normal(factor, right_sides)
    predicted = lax.dot_general(transforms, features, (((0,), (0,)), ((), ())), precision=highest)
    errors = frame_rows - predicted
    pulled = jnp.dot(transforms, errors, precision=highest)
    grad_part = -2.0 * jnp.sum(
        pulled.reshape(bones, 4, local_verts) * homogeneous[None, :, :], axis=1
    )
    error_total = lax.psum(jnp.sum(errors * errors), ("vert", "frame"))
    gradient = lax.psum(grad_part, "frame")
    new_weights = jnp.clip(weights - step_size * gradient, 0.0, 1.0)
    fit_error = error_total / (3.0 * frames_total * verts_total)
    return (new_weights, fit_error)


def solution(mesh):
    placed = (P("frame", None, "vert"), P(None, "vert"), P("vert"), P(None, "vert"))
    return jax.shard_map(
        local, mesh=mesh, in_specs=placed, out_specs=(P(None, "vert"), P()), check_vma=False
    )
```

profile of v0, /device:TPU:1, one launch (start us, length us, event | category | flops | bytes accessed | tf_op | source)
XLA Modules:
  0.0 423.1 jit_solution(11077502006319040849)
XLA Ops:
  7.2 0.0 all-reduce.8.cloned.1.call-start
  7.2 6.0 %copy.19 = f32[128,3,2048]{2,1,0:T(4,128)} copy(f32[128,3,2048]{2,0,1:T(8,128)} %param.4) | data formatting | bytes 6291456 | tf_op args[0]
  13.2 6.0 %reshape.57 = f32[384,2048]{1,0:T(8,128)} reshape(f32[128,3,2048]{2,1,0:T(4,128)} %copy.19) | data formatting | bytes 6291456 | tf_op jit(solution)/shard_map/reshape | solution.py:37
  19.2 0.0 copy-done.2
  19.2 0.0 copy-done.6
  19.2 0.1 fusion.1
  19.3 0.1 fusion
  19.4 0.0 copy-done.7
  19.4 0.0 copy-start.4
  19.4 0.6 copy-done.4
  20.0 1.9 broadcast_multiply_fusion
  22.0 2.0 mul.62
  24.0 0.0 copy-start
  24.0 2.6 fusion.17
  26.5 0.0 copy-done
  26.5 4.3 %fusion.18 = f32[256,384]{1,0:T(8,128)} fusion(f32[256,2048]{1,0:T(8,128)S(1)} %mul.62, f32[384,2048]{1,0:T(8,128)S(1)} %copy-done), kind=kOutput, calls=%fused_computation.49 | convolution fusion | flops 2415919104 | bytes 5636096 | tf_op jit(solution)/shard_map/dot_general | solution.py:39
  30.9 0.0 all-reduce.8.cloned.1.call-update
  30.9 0.2 all-reduce.6.cloned.1.call-start
  31.1 0.6 iota_multiply_fusion
  31.7 196.9 %all-reduce.8.cloned.1.call-done = (f32[256,384]{1,0:T(8,128)}, f32[256,256]{0,1:T(8,128)}) async-done(((f32[256,384]{1,0:T(8,128)}, f32[256,256]{0,1:T(8,128)}), (f32[256,384]{1,0:T(8,128)}, f32[256,256]{0,1:T(8,128)})) %all-reduce.8.cloned.1.call-update) | async-done | bytes 655376 | tf_op jit(solution)/shard_map/psum | solution.py:41
  228.6 1.0 select_add_fusion
  229.6 0.1 copy.14
  229.8 1.0 fusion.3
  230.8 11.7 %cholesky.49 = f32[128,128]{1,0:T(8,128)S(1)} custom-call(f32[128,128]{1,0:T(8,128)S(1)} %cholesky.115), custom_call_target="Cholesky" | custom-call | tf_op jit(solution)/shard_map/jit(cholesky)/cholesky | solution.py:42
  242.5 0.7 copy.15
  243.2 0.6 select_reduce_fusion.1
  243.8 9.8 %custom-call.16 = f32[1,128,128]{1,2,0:T(8,128)S(1)} custom-call(f32[1,128,128]{2,1,0:T(8,128)S(1)} %get-tuple-element.31), custom_call_target="InvertDiagBlocksLowerTriangular" | custom-call | tf_op jit(solution)/shard_map/jit(cholesky)/cholesky | solution.py:42
  253.6 0.2 fusion.6
  253.8 0.7 copy.16
  254.6 0.3 convolution_subtract_fusion.3
  254.8 11.7 %cholesky.103 = f32[128,128]{1,0:T(8,128)S(1)} custom-call(f32[128,128]{1,0:T(8,128)S(1)} %convolution_subtract_fusion.3), custom_call_target="Cholesky" | custom-call | tf_op jit(solution)/shard_map/jit(cholesky)/cholesky | solution.py:42
  266.5 0.1 copy.17
  266.7 0.9 cholesky.111
  267.5 0.8 constant_dynamic-update-slice_fusion.1
  268.4 1.4 compare_reduce_fusion
  271.1 0.7 triangular_solve.69
  271.8 5.4 %while.1 = (s32[]{:T(128)}, f32[256,256]{0,1:T(8,128)S(1)}, s32[2,2]{1,0:T(2,128)S(1)}, f32[2,128,128]{2,1,0:T(8,128)}, s32[]{:T(128)}) while((s32[]{:T(128)}, f32[256,256]{0,1:T(8,128)S(1)}, s32[2,2]{1,0:T(2,128)S(1)}, f32[2,128,128]{2,1,0:T(8,128)}, s32[]{:T(128)}) %tuple.28), condition=%wide.while_cond, body=%wide.while_body.sunk | while | flops 2 | bytes 393329 | solution.py:25
  271.8 0.6 fusion.33
  272.4 1.4 dynamic-slice.7
  273.8 0.1 copy.23
  273.9 0.6 bitcast_dynamic-update-slice_fusion.2
  274.5 0.6 fusion.33
  275.1 1.4 dynamic-slice.7
  276.5 0.1 copy.23
  276.6 0.6 bitcast_dynamic-update-slice_fusion.2
  277.2 20.5 %custom-call.17 = f32[2,128,128]{1,2,0:T(8,128)S(1)} custom-call(f32[2,128,128]{2,1,0:T(8,128)} %get-tuple-element.9), custom_call_target="InvertDiagBlocksLowerTriangular" | custom-call | tf_op jit(solution)/shard_map/triangular_solve | solution.py:25
  297.7 0.0 copy-start.1
  297.7 0.0 copy-done.3
  297.7 0.4 fusion.4
  298.1 0.4 convolution_subtract_fusion.2
  298.5 0.4 fusion.11
  298.9 0.3 fusion.10
  299.2 0.3 convolution_subtract_fusion.1
  299.5 0.3 fusion.9
  299.8 4.1 multiply_reduce_fusion
  304.0 4.9 %fusion.2 = f32[256,2048]{1,0:T(8,128)} fusion(f32[384,2048]{1,0:T(8,128)S(1)} %get-tuple-element.33, f32[128,384]{1,0:T(8,128)S(1)} %fusion.10, f32[128,384]{1,0:T(8,128)S(1)} %fusion.9), kind=kOutput, calls=%fused_computation.15 | convolution fusion | flops 2416017408 | bytes 5636096 | tf_op jit(solution)/shard_map/dot_general | solution.py:46
  308.9 2.1 reshape.58
  311.0 0.0 copy-done.5
  311.0 1.5 multiply_reduce_fusion.1
  312.5 0.8 broadcast_multiply_fusion.1
  313.4 0.0 all-reduce.6.cloned.1.call-update
  313.4 99.1 %psum.31 = f32[]{:T(128)} all-reduce(f32[]{:T(128)} %get-tuple-element.32), channel_id=1, replica_groups=mesh['vert'=64,'frame'=8] {'vert','frame'}, use_global_device_ids=true, to_apply=%region_10.11 | all-reduce | flops 1 | bytes 8 | tf_op jit(solution)/shard_map/psum | solution.py:50
  413.1 0.0 all-reduce.6.cloned.1.call-done
  413.1 2.0 subtract_clamp_fusion
  (14 shorter events, 0.1 us)
Async XLA Ops:
  7.2 221.5 %all-reduce.8.cloned.1.call-start = ((), (), s32[]{:S(2)}) async-start(), calls=%async_computation.1 | async-start | bytes 1310720 | tf_op jit(solution)/shard_map/psum | solution.py:41
  13.2 6.0 %copy-start.2 = (f32[64,2048]{1,0:T(8,128)S(1)}, f32[64,2048]{1,0:T(8,128)}, u32[]{:S(2)}) copy-start(f32[64,2048]{1,0:T(8,128)} %param.7) | copy-start | bytes 1572868
  13.2 6.0 %copy-start.6 = (s32[2048]{0:T(1024)S(1)}, s32[2048]{0:T(1024)}, u32[]{:S(2)}) copy-start(s32[2048]{0:T(1024)} %param.6) | copy-start | bytes 24580
  13.2 6.2 %copy-start.7 = (f32[3,2048]{1,0:T(4,128)S(1)}, f32[3,2048]{1,0:T(4,128)}, u32[]{:S(2)}) copy-start(f32[3,2048]{1,0:T(4,128)} %param.5) | copy-start | bytes 73732
  19.4 0.6 copy-start.4
  24.0 2.6 copy-start
  30.9 382.3 %all-reduce.6.cloned.1.call-start = ((), (), s32[]{:S(2)}) async-start(), calls=%async_computation | async-start | bytes 1048576 | tf_op jit(solution)/shard_map/psum | solution.py:51
  243.2 54.5 %copy-start.3 = (f32[256,384]{1,0:T(8,128)S(1)}, f32[256,384]{1,0:T(8,128)}, u32[]{:S(2)}) copy-start(f32[256,384]{1,0:T(8,128)} %get-tuple-element.26) | copy-start | bytes 1179652
  297.7 2.1 copy-start.1
  308.9 2.1 copy-start.5
Sparse Core Ops, SparseCore 0:
  31.0 197.5 all-reduce.7
  313.5 74.3 all-reduce.5
where the time goes:
time: 424 us; the launch traced here: 423 us
  waiting for transfers between devices  197 us (46%)
  blocking collectives  99.1 us (23%)
  other arithmetic  64.7 us (15%)
  local copies, waits for them, and re-layouts  26.2 us (6%)
  matrix products  18.5 us (4%)
  between operations  17.3 us (4%)
    psum x1, waiting for transfers between devices, local(): gram_matrix, right_sides = lax.psum((gram_part, rhs_part), 'vert')  197 us
    psum x1, blocking collectives, local(): error_total = lax.psum(jnp.sum(errors * errors), ('vert', 'frame'))  99.1 us
    another operation x6, other arithmetic, local(): factor = jnp.linalg.cholesky(gram_matrix + ridge)  35.2 us
    another operation x3, other arithmetic, solve_normal(): lax.linalg.triangular_solve(factor, middle, left_side=True, lower=True, t...  21.1 us
  transfers between devices with their start and end apart: 2, of which 1 were waited for; matrix products, arithmetic and copies ran while one was open for 0% of the time, Pallas kernels for 0%

commit v1 on v0

v1 whole, which is shorter than its diff:
```python
import functools
import jax
import jax.numpy as jnp
from jax import lax
from jax.experimental import pallas as pl
from jax.experimental.pallas import tpu as pltpu
from jax.sharding import PartitionSpec as P

HI = lax.Precision.HIGHEST
NT = (((1,), (1,)), ((), ()))
NN = (((1,), (0,)), ((), ()))
TN = (((0,), (0,)), ((), ()))

def make_weights(lab, prior):
    bones = prior.shape[0]
    ids = lax.broadcasted_iota(jnp.int32, prior.shape, 0)
    summed = jnp.where(ids == lab, 1.0, 0.0) + prior
    return summed / jnp.sum(summed, axis=0, keepdims=True)

def normal_kernel(n_chunk, anim, rest, lab, prior, d_out, w_out, rows, sem):
    n_rows, verts = anim.shape
    bones = prior.shape[0]
    cv = verts // n_chunk
    copies = []
    for j in range(n_chunk):
        cp = pltpu.make_async_copy(anim.at[:, pl.ds(j*cv, cv)], rows.at[:, pl.ds(j*cv, cv)], sem.at[j])
        cp.start()
        copies.append(cp)
    gram = jnp.zeros((4*bones, 4*bones), jnp.float32)
    rhs = jnp.zeros((n_rows, 4*bones), jnp.float32)
    for j in range(n_chunk):
        s = pl.ds(j*cv, cv)
        w = make_weights(lab[:, s], prior[:, s])
        w_out[:, s] = w
        f = jnp.concatenate([w * rest[k:k+1, s] for k in range(3)] + [w], axis=0)
        gram = gram + lax.dot_general(f, f, NT, precision=HI, preferred_element_type=jnp.float32)
        copies[j].wait()
        r = rows[:, s]
        rhs = rhs + lax.dot_general(r, f, NT, precision=HI, preferred_element_type=jnp.float32)
    lanes = 128
    g_tiles = gram.shape[0]//8
    for h in range(2):
        d_out[h*g_tiles:(h+1)*g_tiles] = gram[:, h*lanes:(h+1)*lanes].reshape(g_tiles, 8, lanes)
    r_tiles = rhs.shape[0]//8
    for h in range(2):
        d_out[2*g_tiles+h*r_tiles:2*g_tiles+(h+1)*r_tiles] = rhs[:, h*lanes:(h+1)*lanes].reshape(r_tiles, 8, lanes)

def normal(anim, rest, lab, prior, n_chunk=4):
    n_rows, verts = anim.shape
    bones = prior.shape[0]
    vm = pl.BlockSpec(memory_space=pltpu.VMEM)
    tiles = (4*bones + n_rows)*4*bones//1024
    return pl.pallas_call(
        functools.partial(normal_kernel, n_chunk),
        out_shape=(jax.ShapeDtypeStruct((tiles, 8, 128), jnp.float32), jax.ShapeDtypeStruct((bones, verts), jnp.float32)),
        in_specs=[pl.BlockSpec(memory_space=pltpu.HBM), vm, vm, vm],
        out_specs=(vm, vm),
        scratch_shapes=[pltpu.VMEM((n_rows, verts), jnp.float32), pltpu.SemaphoreType.DMA((n_chunk,))],
        compiler_params=pltpu.CompilerParams(vmem_limit_bytes=40 << 20),
    )(anim, rest, lab.reshape(1, verts), prior)


NX, NY = 4, 8

def vert_id(x, y, core):
    return (x*NY + y)*2 + core

def remote(src, dst, s, r, peer, axis="vert"):
    return pltpu.make_async_remote_copy(src, dst, s, r, device_id={axis: peer}, device_id_type=pl.DeviceIdType.MESH)

def reduce_kernel(d, out, b0, acc, b1, sub, b2, gat, s0, r0, s1, r1, s2, r2, s3, r3, s4, r4, s5, r5):
    me = lax.axis_index("vert")
    core = lax.rem(me, 2)
    y = lax.rem(me//2, NY)
    x = me//(2*NY)
    sib = vert_id(x, y, 1-core)
    xs = [lax.rem(x+k, NX) for k in range(NX)]
    ys = [lax.rem(y+k, NY) for k in range(NY)]
    half = d.shape[0]//2
    q = half//NX
    e = gat.shape[0]//NY
    peers = [sib] + [vert_id(a, y, core) for a in xs[1:]] + [vert_id(x, a, core) for a in ys[1:]]
    barrier = pltpu.get_barrier_semaphore()
    for p in peers:
        pl.semaphore_signal(barrier, inc=1, device_id={"vert": p}, device_id_type=pl.DeviceIdType.MESH)
    pl.semaphore_wait(barrier, len(peers))
    order = (2, 1, 3, 0)
    c0 = []
    for i, k in enumerate(order):
        cp = remote(d.at[pl.ds((1-core)*half + xs[k]*q, q)], b0.at[i], s0.at[i], r0.at[i], sib)
        cp.start()
        c0.append(cp)
    c1 = {}
    for i, k in enumerate(order):
        c0[i].wait_recv()
        acc[i] = b0[i] + d[pl.ds(core*half + xs[k]*q, q)]
        if k:
            c1[k] = remote(acc.at[i], b1.at[k-1], s1.at[k-1], r1.at[k-1], vert_id(xs[k], y, core))
            c1[k].start()
    tot = acc[3]
    for k in (1, 3, 2):
        c1[k].wait_recv()
        tot = tot + b1[k-1]
    sub[0:q] = tot
    sub[q:] = jnp.zeros((sub.shape[0]-q, 8, 128), jnp.float32)
    c2 = {}
    yorder = (4, 3, 5, 2, 6, 1, 7)
    for k in yorder:
        c2[k] = remote(sub.at[pl.ds(ys[k]*e, e)], b2.at[k-1], s2.at[k-1], r2.at[k-1], vert_id(x, ys[k], core))
        c2[k].start()
    tot = sub[pl.ds(y*e, e)]
    for k in yorder[::-1]:
        c2[k].wait_recv()
        tot = tot + b2[k-1]
    gat[pl.ds(y*e, e)] = tot
    c3 = {}
    for k in yorder:
        c3[k] = remote(gat.at[pl.ds(y*e, e)], gat.at[pl.ds(y*e, e)], s3.at[k-1], r3.at[k-1], vert_id(x, ys[k], core))
        c3[k].start()
    for k in yorder[::-1]:
        c3[k].wait_recv()
    mine = pl.ds(core*half + x*q, q)
    out[mine] = gat[0:q]
    c4 = {}
    for k in (2, 1, 3):
        c4[k] = remote(out.at[mine], out.at[mine], s4.at[k-1], r4.at[k-1], vert_id(xs[k], y, core))
        c4[k].start()
    c5 = []
    for i, k in enumerate((0, 1, 3, 2)):
        if k:
            c4[k].wait_recv()
        blk = pl.ds(core*half + lax.rem(x + NX - k, NX)*q, q)
        cp = remote(out.at[blk], out.at[blk], s5.at[i], r5.at[i], sib)
        cp.start()
        c5.append(cp)
    for cp in c5:
        cp.wait_recv()
    for cp in c0 + list(c1.values()) + list(c2.values()) + list(c3.values()) + list(c4.values()) + c5:
        cp.wait_send()

def reduce_vert(d):
    tiles = d.shape[0]
    half = tiles//2
    q = half//NX
    e = -(-q//NY)
    vm = pl.BlockSpec(memory_space=pltpu.VMEM)
    buf = lambda *s: pltpu.VMEM(s + (8, 128), jnp.float32)
    sems = lambda n: [pltpu.SemaphoreType.DMA((n,))]*2
    return pl.pallas_call(
        reduce_kernel, out_shape=jax.ShapeDtypeStruct(d.shape, d.dtype), in_specs=[vm], out_specs=vm,
        scratch_shapes=[buf(NX, q), buf(NX, q), buf(NX-1, q), buf(NY*e), buf(NY-1, e), buf(NY*e)]
        + sems(4) + sems(3) + sems(7) + sems(7) + sems(3) + sems(4),
        compiler_params=pltpu.CompilerParams(collective_id=0, has_side_effects=True, vmem_limit_bytes=24 << 20),
        name="reduce_vert",
    )(d)


ridge_scale = 0.0001
step_size = 0.005

def hdot(a, b, dims=NN):
    return lax.dot_general(a, b, dims, precision=HI, preferred_element_type=jnp.float32)

def sweep_small(p):
    n = p.shape[0]
    sub = lax.broadcasted_iota(jnp.int32, (n, 1), 0)
    lane = lax.broadcasted_iota(jnp.int32, (1, n), 1)
    for k in range(n):
        row, col = p[k:k+1, :], p[:, k:k+1]
        inv = 1.0/p[k:k+1, k:k+1]
        colp = jnp.where(sub == k, -1.0, col)
        wp = jnp.where(lane == k, -1.0, row)*inv
        p = jnp.where((sub == k) | (lane == k), 0.0, p) - colp*wp
    return p

def negative_inverse(a, nb=32):
    n = a.shape[0]
    sub = lax.broadcasted_iota(jnp.int32, (n, n), 0)//nb
    lane = lax.broadcasted_iota(jnp.int32, (n, n), 1)//nb
    eye = (lax.broadcasted_iota(jnp.int32, (nb, nb), 0) == lax.broadcasted_iota(jnp.int32, (nb, nb), 1)).astype(jnp.float32)
    for i in range(n//nb):
        s = i*nb
        rows = a[s:s+nb]
        neg = sweep_small(rows[:, s:s+nb])
        w = -hdot(neg, rows)
        parts = lambda mid, full: jnp.concatenate(([full[:, :s]] if s else []) + [mid] + ([full[:, s+nb:]] if s+nb < n else []), axis=1)
        a = jnp.where((sub == i) | (lane == i), 0.0, a) - hdot(parts(-eye, rows), parts(neg, w), TN)
    return a

def fit_kernel(n_chunk, ridge, anim, d, rest, w_ref, g_out, e_out, rows, sem):
    n_rows, verts = anim.shape
    bones = w_ref.shape[0]
    joint = 4*bones
    cv = verts // n_chunk
    copies = []
    for j in range(n_chunk):
        cp = pltpu.make_async_copy(anim.at[:, pl.ds(j*cv, cv)], rows.at[:, pl.ds(j*cv, cv)], sem.at[j])
        cp.start()
        copies.append(cp)
    gt, rt = joint//8, n_rows//8
    eye = lax.broadcasted_iota(jnp.int32, (joint, joint), 0) == lax.broadcasted_iota(jnp.int32, (joint, joint), 1)
    gram = jnp.concatenate([d[h*gt:(h+1)*gt].reshape(joint, 128) for h in range(2)], axis=1)
    gram = gram + jnp.where(eye, ridge, 0.0)
    rhs = jnp.concatenate([d[2*gt+h*rt:2*gt+(h+1)*rt].reshape(n_rows, 128) for h in range(2)], axis=1)
    neg = negative_inverse(gram)
    tt = -hdot(rhs, neg)
    tt = tt - hdot(rhs - hdot(tt, gram), neg)
    t = tt.T
    total = jnp.zeros((8, 128), jnp.float32)
    for j in range(n_chunk):
        s = pl.ds(j*cv, cv)
        w = w_ref[:, s]
        h = [rest[k:k+1, s] for k in range(3)]
        f = jnp.concatenate([w * h[k] for k in range(3)] + [w], axis=0)
        copies[j].wait()
        r = rows[:, s]
        e = r - hdot(tt, f)
        sq = (e*e).reshape(n_rows//8, 8, cv).sum(axis=0)
        for q in range(cv//128):
            total = total + sq[:, q*128:(q+1)*128]
        pulled = hdot(t, e)
        grad = pulled[3*bones:]
        for k in range(3):
            grad = grad + pulled[k*bones:(k+1)*bones]*h[k]
        g_out[:, :, s] = (-2.0*grad).reshape(bones//8, 8, cv)
    e_out[0] = total

def fit(anim, d, rest, w, verts_total, n_chunk=4):
    n_rows, verts = anim.shape
    bones = w.shape[0]
    vm = pl.BlockSpec(memory_space=pltpu.VMEM)
    return pl.pallas_call(
        functools.partial(fit_kernel, n_chunk, ridge_scale*verts_total),
        out_shape=(jax.ShapeDtypeStruct((bones//8, 8, verts), jnp.float32), jax.ShapeDtypeStruct((1, 8, 128), jnp.float32)),
        in_specs=[pl.BlockSpec(memory_space=pltpu.HBM), vm, vm, vm],
        out_specs=(vm, vm),
        scratch_shapes=[pltpu.VMEM((n_rows, verts), jnp.float32), pltpu.SemaphoreType.DMA((n_chunk,))],
        compiler_params=pltpu.CompilerParams(vmem_limit_bytes=40 << 20),
        name="fit",
    )(anim, d, rest, w)


def frame_kernel(scale, g, e, w, out, f_out, gb, ez, ey, ex, ec, et, sg, rg, sa, ra, sz, rz, sy, ry, sx, rx, sc, rc):
    me = lax.axis_index("vert")
    z = lax.axis_index("frame")
    nz = g.shape[0]
    core = lax.rem(me, 2)
    y = lax.rem(me//2, NY)
    x = me//(2*NY)
    sib = vert_id(x, y, 1-core)
    zs = [lax.rem(z+k, nz) for k in range(nz)]
    xs = [vert_id(lax.rem(x+k, NX), y, core) for k in range(NX)]
    ys = [vert_id(x, lax.rem(y+k, NY), core) for k in range(NY)]
    barrier = pltpu.get_barrier_semaphore()
    for p in [sib] + xs[1:] + ys[1:]:
        pl.semaphore_signal(barrier, inc=1, device_id={"vert": p}, device_id_type=pl.DeviceIdType.MESH)
    for p in zs[1:]:
        pl.semaphore_signal(barrier, inc=1, device_id={"frame": p}, device_id_type=pl.DeviceIdType.MESH)
    pl.semaphore_wait(barrier, 1 + NX-1 + NY-1 + nz-1)
    order = (4, 3, 5, 2, 6, 1, 7)
    cz = [remote(e.at[0], ez.at[k-1], sz.at[k-1], rz.at[k-1], zs[k], "frame") for k in order]
    for cp in cz:
        cp.start()
    cg = [remote(g.at[zs[k]], gb.at[k-1], sg.at[k-1], rg.at[k-1], zs[k], "frame") for k in order]
    for cp in cg:
        cp.start()
    for cp in cz:
        cp.wait_recv()
    tot = e[0]
    for k in range(1, nz):
        tot = tot + ez[k-1]
    et[0] = tot
    cy = [remote(et.at[0], ey.at[k-1], sy.at[k-1], ry.at[k-1], ys[k]) for k in order]
    for cp in cy:
        cp.start()
    for cp in cy:
        cp.wait_recv()
    tot = et[0]
    for k in range(1, NY):
        tot = tot + ey[k-1]
    et[1] = tot
    cx = [remote(et.at[1], ex.at[k-1], sx.at[k-1], rx.at[k-1], xs[k]) for k in (2, 1, 3)]
    for cp in cx:
        cp.start()
    for cp in cx:
        cp.wait_recv()
    tot = et[1]
    for k in range(1, NX):
        tot = tot + ex[k-1]
    et[2] = tot
    cc = remote(et.at[2], ec.at[0], sc.at[0], rc.at[0], sib)
    cc.start()
    grad = g[z]
    for cp, k in zip(cg[::-1], order[::-1]):
        cp.wait_recv()
        grad = grad + gb[k-1]
    out[z] = jnp.clip(w[z] - step_size*grad, 0.0, 1.0)
    ca = [remote(out.at[z], out.at[z], sa.at[k-1], ra.at[k-1], zs[k], "frame") for k in order]
    for cp in ca:
        cp.start()
    cc.wait_recv()
    f_out[...] = jnp.sum(et[2] + ec[0], axis=(0, 1), keepdims=True)*scale
    for cp in ca:
        cp.wait_recv()
    for cp in cz + cg + cy + cx + [cc] + ca:
        cp.wait_send()

def reduce_frame(g, e, w, scale):
    nz, eight, verts = g.shape
    vm = pl.BlockSpec(memory_space=pltpu.VMEM)
    buf = lambda *s: pltpu.VMEM(s + (8, 128), jnp.float32)
    sems = lambda n: [pltpu.SemaphoreType.DMA((n,))]*2
    return pl.pallas_call(
        functools.partial(frame_kernel, scale),
        out_shape=(jax.ShapeDtypeStruct(g.shape, g.dtype), jax.ShapeDtypeStruct((1, 1), jnp.float32)),
        in_specs=[vm, vm, vm], out_specs=(vm, vm),
        scratch_shapes=[pltpu.VMEM((nz-1, eight, verts), jnp.float32), buf(nz-1), buf(NY-1), buf(NX-1), buf(1), buf(3)]
        + sems(nz-1) + sems(nz-1) + sems(nz-1) + sems(NY-1) + sems(NX-1) + sems(1),
        compiler_params=pltpu.CompilerParams(collective_id=1, has_side_effects=True, vmem_limit_bytes=24 << 20),
        name="reduce_frame",
    )(g, e, w)


def local(animated, rest_positions, labels, weight_prior):
    bones, local_verts = weight_prior.shape
    verts_total = local_verts * lax.axis_size("vert")
    frames_total = animated.shape[0] * lax.axis_size("frame")
    rows = animated.transpose(1, 0, 2).reshape(-1, local_verts)
    sums, weights = normal(rows, rest_positions, labels, weight_prior)
    sums = reduce_vert(sums)
    grad, squares = fit(rows, sums, rest_positions, weights, verts_total)
    scale = 1.0 / (3.0 * frames_total * verts_total)
    new_weights, fit_error = reduce_frame(grad, squares, weights.reshape(grad.shape), scale)
    return new_weights.reshape(bones, local_verts), fit_error.reshape(())


def solution(mesh):
    placed = (P("frame", None, "vert"), P(None, "vert"), P("vert"), P(None, "vert"))
    return jax.shard_map(
        local, mesh=mesh, in_specs=placed, out_specs=(P(None, "vert"), P()), check_vma=False
    )
```

time: 424 us -> 121 us (0.29)
  waiting for transfers between devices: 197 us -> 0 us
  Pallas kernels: 0 us -> 113 us
  blocking collectives: 99.1 us -> 0 us
  other arithmetic: 64.7 us -> 0 us
  local copies, waits for them, and re-layouts: 26.2 us -> 5.17 us
  matrix products: 18.5 us -> 0 us
  between operations: 17.3 us -> 2.49 us
    psum x2 -> x0, waiting for transfers between devices: 197 us -> none  [the longest x1 197 us: local(): gram_matrix, right_sides = lax.psum((gram_part, rhs_part), 'vert')]
    pallas_call x0 -> x4, Pallas kernels: none -> 113 us  [the longest x1 38.1 us: reduce_frame(): pl.pallas_call(functools.partial(frame_kernel, scale), out_shape=(jax.Sha...]
    psum x1 -> x0, blocking collectives: 99.1 us -> none  [local(): error_total = lax.psum(jnp.sum(errors * errors), ('vert', 'frame'))]
    another operation x9 -> x0, other arithmetic: 56.3 us -> none  [the longest x6 35.2 us: local(): factor = jnp.linalg.cholesky(gram_matrix + ridge)]
    dot_general x4 -> x0, matrix products: 15.9 us -> none  [the longest x1 4.92 us: local(): pulled = jnp.dot(transforms, errors, precision=highest)]
    another operation x18 -> x0, local copies, waits for them, and re-layouts: 9.37 us -> none
    reshape x2 -> x0, local copies, waits for them, and re-layouts: 8.15 us -> none  [the longest x1 6.02 us: local(): frame_rows = animated.reshape(-1, local_verts)]
  transfers between devices with their start and end apart: 2 -> 0, of which waited for: 1 -> 0; matrix products, arithmetic and copies ran while one was open for 0% -> 0% of each run, Pallas kernels for 0% -> 0%
where the time goes in v1:
time: 121 us
  Pallas kernels  113 us (93%)
  local copies, waits for them, and re-layouts  5.17 us (4%)
  between operations  2.49 us (2%)
    pallas_call x1, Pallas kernels, reduce_frame(): pl.pallas_call(functools.partial(frame_kernel, scale), out_shape=(jax.Sha...  38.1 us
    pallas_call x1, Pallas kernels, fit(): pl.pallas_call(functools.partial(fit_kernel, n_chunk, ridge_scale * verts...  36.5 us
    pallas_call x1, Pallas kernels, reduce_vert(): pl.pallas_call(reduce_kernel, out_shape=jax.ShapeDtypeStruct(d.shape, d.d...  32 us
    pallas_call x1, Pallas kernels, normal(): pl.pallas_call(functools.partial(normal_kernel, n_chunk), out_shape=(jax....  6.67 us
    unnamed x9, local copies, waits for them, and re-layouts  5.17 us

profile of v1, /device:TPU:1, one launch (start us, length us, event | category | flops | bytes accessed | tf_op | source)
XLA Modules:
  0.0 120.9 jit_solution(13300770596532207593)
XLA Ops:
  0.6 0.0 copy-start
  0.6 1.9 %copy-done = f32[128,3,2048]{2,0,1:T(8,128)S(1)} copy-done((f32[128,3,2048]{2,0,1:T(8,128)S(1)}, f32[128,3,2048]{2,0,1:T(8,128)}, u32[]{:S(2)}) %copy-start) | copy-done | bytes 3145752
  2.5 0.0 copy-start.1
  2.5 1.0 copy-done.1
  3.6 0.0 copy-start.2
  3.6 0.8 copy-done.2
  4.3 0.0 copy-start.3
  4.3 0.7 copy-done.3
  5.0 6.7 %shard_map.59 = (f32[160,8,128]{2,1,0:T(8,128)S(1)}, f32[64,2048]{1,0:T(8,128)S(1)}) custom-call(f32[384,2048]{1,0:T(8,128)S(1)} %bitcast.7, f32[3,2048]{1,0:T(4,128)S(1)} %copy-done.2, s32[1,2048]{1,0:T(1,128)S(1)} %bitcast.11, f32[64,2048]{1,0:T(8,128)S(1)} %copy-done.1), custom_call_target="tpu_custom_call" | custom-call | tf_op jit(solution)/shard_map/pallas_call | solution.py:53
  11.7 32.0 %reduce_vert.1.d = f32[160,8,128]{2,1,0:T(8,128)S(1)} custom-call(f32[160,8,128]{2,1,0:T(8,128)S(1)} %get-tuple-element.8.d), custom_call_target="tpu_custom_call" | custom-call | tf_op jit(solution)/shard_map/reduce_vert/pallas_call | solution.py:149
  43.7 36.5 %fit.1 = (f32[8,8,2048]{2,1,0:T(8,128)S(1)}, f32[1,8,128]{2,1,0:T(8,128)S(1)}) custom-call(f32[384,2048]{1,0:T(8,128)S(1)} %bitcast.8, f32[160,8,128]{2,1,0:T(8,128)S(1)} %reduce_vert.1.d, f32[3,2048]{1,0:T(4,128)S(1)} %copy-done.2, f32[64,2048]{1,0:T(8,128)S(1)} %get-tuple-element.9.w_ref), custom_call_target="tpu_custom_call" | custom-call | tf_op jit(solution)/shard_map/fit/pallas_call | solution.py:232
  80.2 38.1 %reduce_frame.1 = (f32[8,8,2048]{2,1,0:T(8,128)S(1)}, f32[1,1]{1,0:T(1,128)}) custom-call(f32[8,8,2048]{2,1,0:T(8,128)S(1)} %get-tuple-element.10.g, f32[1,8,128]{2,1,0:T(8,128)S(1)} %get-tuple-element.11.e, f32[8,8,2048]{2,1,0:T(8,128)S(1)} %bitcast.9), custom_call_target="tpu_custom_call" | custom-call | tf_op jit(solution)/shard_map/reduce_frame/pallas_call | solution.py:313
  118.3 0.8 copy.8
Async XLA Ops:
  0.6 1.9 %copy-start = (f32[128,3,2048]{2,0,1:T(8,128)S(1)}, f32[128,3,2048]{2,0,1:T(8,128)}, u32[]{:S(2)}) copy-start(f32[128,3,2048]{2,0,1:T(8,128)} %param.4) | copy-start | bytes 9437188
  2.5 1.0 copy-start.1
  3.6 0.8 copy-start.2
  4.3 0.7 copy-start.3

commit v2 on v0

v2 whole, which is shorter than its diff:
```python
import functools

import jax
import jax.numpy as jnp
from jax import lax
from jax.experimental import pallas as pl
from jax.experimental.pallas import tpu as pltpu
from jax.sharding import PartitionSpec as P

HI = lax.Precision.HIGHEST
MESH = pl.DeviceIdType.MESH
NT = (((1,), (1,)), ((), ()))
NN = (((1,), (0,)), ((), ()))
TN = (((0,), (0,)), ((), ()))
NX, NY, NZ = 4, 8, 8
CHUNKS = 4
ridge_scale = 0.0001
step_size = 0.005
far_first = (4, 3, 5, 2, 6, 1, 7)


def hdot(a, b, dims=NN):
    return lax.dot_general(a, b, dims, precision=HI, preferred_element_type=jnp.float32)


def sym(f, n):
    m = [[None] * n for _ in range(n)]
    for i in range(n):
        for j in range(i, n):
            m[i][j] = m[j][i] = f(i, j)
    return m


def total(terms):
    while len(terms) > 1:
        terms = [terms[i] + terms[i + 1] for i in range(0, len(terms) - 1, 2)] + (
            [terms[-1]] if len(terms) % 2 else []
        )
    return terms[0]


def inv_sym(m):
    n = len(m)
    if n == 2:
        r = 1.0 / (m[0][0] * m[1][1] - m[0][1] * m[0][1])
        b = -m[0][1] * r
        return [[m[1][1] * r, b], [b, m[0][0] * r]]
    h = n // 2
    rng = range(h)
    a = inv_sym([row[:h] for row in m[:h]])
    f = [row[h:] for row in m[:h]]
    af = [[total([a[i][l] * f[l][j] for l in rng]) for j in rng] for i in rng]
    s = inv_sym(sym(lambda i, j: m[h + i][h + j] - total([f[l][i] * af[l][j] for l in rng]), h))
    off = [[-total([af[i][l] * s[l][j] for l in rng]) for j in rng] for i in rng]
    top = sym(lambda i, j: a[i][j] - total([off[i][l] * af[j][l] for l in rng]), h)
    return [top[i] + off[i] for i in rng] + [[off[j][i] for j in rng] + s[i] for i in rng]


def sweep(p, b):
    n = p.shape[0]
    sub = lax.broadcasted_iota(jnp.int32, (n, n), 0)
    lane = lax.broadcasted_iota(jnp.int32, (n, n), 1)
    lane1 = lane[0:1]
    for k in range(0, n, b):
        c = [jnp.broadcast_to(p[:, k + j : k + j + 1], (n, n)) for j in range(b)]
        m = inv_sym(sym(lambda i, j: c[j][k + i : k + i + 1], b))
        r = [
            jnp.where(lane1 == k + j, -1.0, jnp.where(lane1 // b == k // b, 0.0, p[k + j : k + j + 1]))
            for j in range(b)
        ]
        w = [total([m[i][j] * r[j] for j in range(b)]) for i in range(b)]
        c = [jnp.where(sub == k + j, -1.0, jnp.where(sub // b == k // b, 0.0, c[j])) for j in range(b)]
        keep = jnp.where((sub // b == k // b) | (lane // b == k // b), 0.0, p)
        p = keep - total([c[j] * w[j] for j in range(b)])
    return p


def negative_inverse(a, nb, b, between):
    n = a.shape[0]
    sub = lax.broadcasted_iota(jnp.int32, (n, n), 0) // nb
    lane = lax.broadcasted_iota(jnp.int32, (n, n), 1) // nb
    square = (nb, nb)
    eye = (
        lax.broadcasted_iota(jnp.int32, square, 0) == lax.broadcasted_iota(jnp.int32, square, 1)
    ).astype(jnp.float32)
    for i in range(n // nb):
        s = i * nb
        rows = a[s : s + nb]
        neg = sweep(rows[:, s : s + nb], b)
        w = -hdot(neg, rows)

        def parts(middle, full):
            left = [full[:, :s]] if s else []
            right = [full[:, s + nb :]] if s + nb < n else []
            return jnp.concatenate(left + [middle] + right, axis=1)

        a = jnp.where((sub == i) | (lane == i), 0.0, a) - hdot(parts(-eye, rows), parts(neg, w), TN)
        between(i)
    return a


class Place:
    def __init__(self):
        me = lax.axis_index("vert")
        self.core = lax.rem(me, 2)
        self.y = lax.rem(me // 2, NY)
        self.x = me // (2 * NY)
        self.z = lax.axis_index("frame")
        self.xs = [lax.rem(self.x + k, NX) for k in range(NX)]
        self.ys = [lax.rem(self.y + k, NY) for k in range(NY)]
        self.zs = [lax.rem(self.z + k, NZ) for k in range(NZ)]
        vert = lambda x, y, core: {"vert": (x * NY + y) * 2 + core}
        self.sib = vert(self.x, self.y, 1 - self.core)
        self.xp = [vert(a, self.y, self.core) for a in self.xs]
        self.yp = [vert(self.x, a, self.core) for a in self.ys]
        self.zp = [{"frame": a} for a in self.zs]


def send(src, dst, s, r, peer):
    cp = pltpu.make_async_remote_copy(src, dst, s, r, device_id=peer, device_id_type=MESH)
    cp.start()
    return cp


def reduce_steps(pos, d, bufs, sems, sent):
    b0, acc, b1, sub, b2, gat, full = bufs
    (s0, r0), (s1, r1), (s2, r2), (s3, r3), (s4, r4), (s5, r5) = sems
    half = d.shape[0] // 2
    q = half // NX
    e = gat.shape[0] // NY
    xs, ys, core = pos.xs, pos.ys, pos.core
    order = (2, 1, 3, 0)
    c0 = [
        send(d.at[pl.ds((1 - core) * half + xs[k] * q, q)], b0.at[i], s0.at[i], r0.at[i], pos.sib)
        for i, k in enumerate(order)
    ]
    sent += c0
    yield
    c1 = {}
    for i, k in enumerate(order):
        c0[i].wait_recv()
        acc[i] = b0[i] + d[pl.ds(core * half + xs[k] * q, q)]
        if k:
            c1[k] = send(acc.at[i], b1.at[k - 1], s1.at[k - 1], r1.at[k - 1], pos.xp[k])
    sent += c1.values()
    yield
    tot = acc[3]
    for k in (1, 3, 2):
        c1[k].wait_recv()
        tot = tot + b1[k - 1]
    sub[0:q] = tot
    if NY * e > q:
        sub[q:] = jnp.zeros((NY * e - q, 8, 128), jnp.float32)
    c2 = {
        k: send(sub.at[pl.ds(ys[k] * e, e)], b2.at[k - 1], s2.at[k - 1], r2.at[k - 1], pos.yp[k])
        for k in far_first
    }
    sent += c2.values()
    yield
    mine = pl.ds(pos.y * e, e)
    tot = sub[mine]
    for k in far_first[::-1]:
        c2[k].wait_recv()
        tot = tot + b2[k - 1]
    gat[mine] = tot
    c3 = {
        k: send(gat.at[mine], gat.at[mine], s3.at[k - 1], r3.at[k - 1], pos.yp[k]) for k in far_first
    }
    sent += c3.values()
    yield
    for k in far_first[::-1]:
        c3[k].wait_recv()
    mine = pl.ds(core * half + pos.x * q, q)
    full[mine] = gat[0:q]
    c4 = {k: send(full.at[mine], full.at[mine], s4.at[k - 1], r4.at[k - 1], pos.xp[k]) for k in (2, 1, 3)}
    c5 = [send(full.at[mine], full.at[mine], s5.at[0], r5.at[0], pos.sib)]
    sent += c4.values()
    yield
    for i, k in enumerate((1, 3, 2)):
        c4[k].wait_recv()
        blk = pl.ds(core * half + lax.rem(pos.x + NX - k, NX) * q, q)
        c5.append(send(full.at[blk], full.at[blk], s5.at[i + 1], r5.at[i + 1], pos.sib))
    sent += c5
    yield
    for cp in c5:
        cp.wait_recv()
    yield


def kernel(ridge, scale, *refs):
    it = iter(refs)
    take = lambda n: [next(it) for _ in range(n)]
    anim, rest_h, lab_h, prior_h, out, f_out = take(6)
    rows, feats, rest, lab, w_ref, dg, dr, g, gb = take(9)
    ez, ey, ex, ec, et = take(5)
    g_bufs, r_bufs = take(7), take(7)
    in_sem, row_sem = take(2)
    pairs = lambda n: [tuple(take(2)) for _ in range(n)]
    g_sems, r_sems = pairs(6), pairs(6)
    (sg, rg), (sa, ra), (sz, rz), (sy, ry), (sx, rx), (sc, rc) = pairs(6)

    n_rows, verts = anim.shape
    bones = prior_h.shape[0]
    joint = 4 * bones
    cv = verts // CHUNKS
    pos = Place()

    small = [
        pltpu.make_async_copy(src, dst, in_sem.at[i])
        for i, (src, dst) in enumerate(((prior_h, w_ref), (rest_h, rest), (lab_h, lab)))
    ]
    for cp in small:
        cp.start()
    for j in range(CHUNKS):
        s = pl.ds(j * cv, cv)
        pltpu.make_async_copy(anim.at[:, s], rows.at[:, s], row_sem.at[j]).start()
    barrier = pltpu.get_barrier_semaphore()
    peers = [pos.sib] + pos.xp[1:] + pos.yp[1:] + pos.zp[1:]
    for p in peers:
        pl.semaphore_signal(barrier, inc=1, device_id=p, device_id_type=MESH)
    for cp in small:
        cp.wait()

    ids = lax.broadcasted_iota(jnp.int32, (bones, cv), 0)

    def gram_chunk(j, gram):
        s = pl.ds(pl.multiple_of(j * cv, cv), cv)
        summed = jnp.where(ids == lab[:, s], 1.0, 0.0) + w_ref[:, s]
        w = summed / jnp.sum(summed, axis=0, keepdims=True)
        w_ref[:, s] = w
        f = jnp.concatenate([w * rest[k : k + 1, s] for k in range(3)] + [w], axis=0)
        feats[:, s] = f
        return gram + hdot(f, f, NT)

    gram = lax.fori_loop(0, CHUNKS, gram_chunk, jnp.zeros((joint, joint), jnp.float32))
    gt, rt = joint // 8, n_rows // 8
    for h in range(2):
        dg[h * gt : (h + 1) * gt] = gram[:, h * 128 : (h + 1) * 128].reshape(gt, 8, 128)
    sent = []
    pl.semaphore_wait(barrier, len(peers))
    gsteps = reduce_steps(pos, dg, g_bufs, g_sems, sent)
    rsteps = reduce_steps(pos, dr, r_bufs, r_sems, sent)
    next(gsteps)

    def rhs_chunk(j, rhs):
        s = pl.ds(pl.multiple_of(j * cv, cv), cv)
        pltpu.make_async_copy(anim.at[:, s], rows.at[:, s], row_sem.at[j]).wait()
        return rhs + hdot(rows[:, s], feats[:, s], NT)

    next(gsteps)
    rhs = lax.fori_loop(0, CHUNKS, rhs_chunk, jnp.zeros((n_rows, joint), jnp.float32))
    for h in range(2):
        dr[h * rt : (h + 1) * rt] = rhs[:, h * 128 : (h + 1) * 128].reshape(rt, 8, 128)
    next(rsteps)
    next(gsteps)
    next(rsteps)
    next(gsteps)
    next(rsteps)
    next(gsteps)
    next(rsteps)
    next(gsteps)
    next(gsteps)

    square = (joint, joint)
    eye = lax.broadcasted_iota(jnp.int32, square, 0) == lax.broadcasted_iota(jnp.int32, square, 1)
    dg, dr = g_bufs[-1], r_bufs[-1]
    gram = jnp.concatenate([dg[h * gt : (h + 1) * gt].reshape(joint, 128) for h in range(2)], axis=1)
    gram = gram + jnp.where(eye, ridge, 0.0)
    neg = negative_inverse(gram, 64, 4, lambda i: next(rsteps) if i < 3 else None)
    rhs = jnp.concatenate([dr[h * rt : (h + 1) * rt].reshape(n_rows, 128) for h in range(2)], axis=1)
    tt = -hdot(rhs, neg)
    tt = tt - hdot(rhs - hdot(tt, gram), neg)
    t = tt.T

    def fit_chunk(j, squares):
        s = pl.ds(pl.multiple_of(j * cv, cv), cv)
        e = rows[:, s] - hdot(tt, feats[:, s])
        pulled = hdot(t, e)
        grad = pulled[3 * bones :]
        for k in range(3):
            grad = grad + pulled[k * bones : (k + 1) * bones] * rest[k : k + 1, s]
        g[:, :, s] = (-2.0 * grad).reshape(NZ, bones // NZ, cv)
        for k in far_first:
            send(g.at[pos.zs[k], :, s], gb.at[k - 1, :, s], sg.at[j, k - 1], rg.at[j, k - 1], pos.zp[k])
        sq = (e * e).reshape(n_rows // 8, 8, cv).sum(axis=0)
        return squares + total([sq[:, i * 128 : (i + 1) * 128] for i in range(cv // 128)])

    et[0] = lax.fori_loop(0, CHUNKS, fit_chunk, jnp.zeros((8, 128), jnp.float32))
    cz = [send(et.at[0], ez.at[k - 1], sz.at[k - 1], rz.at[k - 1], pos.zp[k]) for k in far_first]

    mine = pl.ds(pl.multiple_of(pos.z * (bones // NZ), bones // NZ), bones // NZ)

    def update_chunk(j, carry):
        s = pl.ds(pl.multiple_of(j * cv, cv), cv)
        grad = g[pos.z, :, s]
        for k in far_first[::-1]:
            pltpu.make_async_remote_copy(
                g.at[pos.zs[k], :, s], gb.at[k - 1, :, s], sg.at[j, k - 1], rg.at[j, k - 1],
                device_id=pos.zp[k], device_id_type=MESH,
            ).wait()
            grad = grad + gb[k - 1, :, s]
        out[pos.z, :, s] = jnp.clip(w_ref[mine, s] - step_size * grad, 0.0, 1.0)
        for k in far_first:
            send(out.at[pos.z, :, s], out.at[pos.z, :, s], sa.at[j, k - 1], ra.at[j, k - 1], pos.zp[k])
        return carry

    lax.fori_loop(0, CHUNKS, update_chunk, 0)

    def add_up(copies, buf, i):
        tot = et[i]
        for cp in copies:
            cp.wait_recv()
        for k in range(buf.shape[0]):
            tot = tot + buf[k]
        et[i + 1] = tot

    add_up(cz, ez, 0)
    cy = [send(et.at[1], ey.at[k - 1], sy.at[k - 1], ry.at[k - 1], pos.yp[k]) for k in far_first]
    add_up(cy, ey, 1)
    cx = [send(et.at[2], ex.at[k - 1], sx.at[k - 1], rx.at[k - 1], pos.xp[k]) for k in (2, 1, 3)]
    add_up(cx, ex, 2)
    cc = [send(et.at[3], ec.at[0], sc.at[0], rc.at[0], pos.sib)]
    add_up(cc, ec, 3)
    f_out[...] = jnp.sum(et[4], axis=(0, 1), keepdims=True) * scale

    def gather_chunk(j, carry):
        s = pl.ds(pl.multiple_of(j * cv, cv), cv)
        for k in far_first[::-1]:
            pltpu.make_async_remote_copy(
                out.at[pos.z, :, s], out.at[pos.z, :, s], sa.at[j, k - 1], ra.at[j, k - 1],
                device_id=pos.zp[k], device_id_type=MESH,
            ).wait()
        return carry

    lax.fori_loop(0, CHUNKS, gather_chunk, 0)
    for cp in sent + cz + cy + cx + cc:
        cp.wait_send()


def local(animated, rest_positions, labels, weight_prior):
    bones, verts = weight_prior.shape
    n_rows = 3 * animated.shape[0]
    joint = 4 * bones
    verts_total = verts * lax.axis_size("vert")
    frames_total = animated.shape[0] * lax.axis_size("frame")
    rows = animated.transpose(1, 0, 2).reshape(n_rows, verts)

    vmem = lambda *s: pltpu.VMEM(s, jnp.float32)
    tiles = lambda *s: vmem(*s, 8, 128)

    def buffers(n):
        q = n // (2 * NX)
        e = -(-q // NY)
        return [tiles(NX, q), tiles(NX, q), tiles(NX - 1, q), tiles(NY * e), tiles(NY - 1, e), tiles(NY * e), tiles(n)]

    pair = lambda *s: [pltpu.SemaphoreType.DMA(s)] * 2
    reduce_pairs = pair(4) + pair(3) + pair(7) + pair(7) + pair(3) + pair(4)
    n_gram, n_rhs = joint * joint // 1024, n_rows * joint // 1024
    scratch = [
        vmem(n_rows, verts), vmem(joint, verts), vmem(3, verts), pltpu.VMEM((1, verts), jnp.int32),
        vmem(bones, verts), tiles(n_gram), tiles(n_rhs), vmem(NZ, bones // NZ, verts),
        vmem(NZ - 1, bones // NZ, verts), tiles(NZ - 1), tiles(NY - 1), tiles(NX - 1), tiles(1), tiles(5),
    ]
    scratch += buffers(n_gram) + buffers(n_rhs)
    scratch += [pltpu.SemaphoreType.DMA((3,)), pltpu.SemaphoreType.DMA((CHUNKS,))]
    scratch += reduce_pairs + reduce_pairs
    scratch += pair(CHUNKS, NZ - 1) + pair(CHUNKS, NZ - 1) + pair(NZ - 1) + pair(NY - 1) + pair(NX - 1) + pair(1)

    hbm, vm = pl.BlockSpec(memory_space=pltpu.HBM), pl.BlockSpec(memory_space=pltpu.VMEM)
    new_weights, fit_error = pl.pallas_call(
        functools.partial(kernel, ridge_scale * verts_total, 1.0 / (3.0 * frames_total * verts_total)),
        out_shape=(
            jax.ShapeDtypeStruct((NZ, bones // NZ, verts), jnp.float32),
            jax.ShapeDtypeStruct((1, 1), jnp.float32),
        ),
        in_specs=[hbm] * 4,
        out_specs=(vm, vm),
        scratch_shapes=scratch,
        compiler_params=pltpu.CompilerParams(
            collective_id=0, has_side_effects=True, vmem_limit_bytes=56 << 20
        ),
        name="skinning",
    )(rows, rest_positions, labels.reshape(1, verts), weight_prior)
    return new_weights.reshape(bones, verts), fit_error.reshape(())


def solution(mesh):
    placed = (P("frame", None, "vert"), P(None, "vert"), P("vert"), P(None, "vert"))
    return jax.shard_map(
        local, mesh=mesh, in_specs=placed, out_specs=(P(None, "vert"), P()), check_vma=False
    )
```

time: 424 us -> 90.5 us (0.21)
  waiting for transfers between devices: 197 us -> 0 us
  blocking collectives: 99.1 us -> 0 us
  Pallas kernels: 0 us -> 86.1 us
  other arithmetic: 64.7 us -> 0 us
  local copies, waits for them, and re-layouts: 26.2 us -> 1.87 us
  matrix products: 18.5 us -> 0 us
  between operations: 17.3 us -> 2.34 us
    psum x2 -> x0, waiting for transfers between devices: 197 us -> none  [the longest x1 197 us: local(): gram_matrix, right_sides = lax.psum((gram_part, rhs_part), 'vert')]
    psum x1 -> x0, blocking collectives: 99.1 us -> none  [local(): error_total = lax.psum(jnp.sum(errors * errors), ('vert', 'frame'))]
    pallas_call x0 -> x1, Pallas kernels: none -> 86.1 us  [local(): pl.pallas_call(functools.partial(kernel, ridge_scale * verts_total, 1.0 /...]
    another operation x9 -> x0, other arithmetic: 56.3 us -> none  [the longest x6 35.2 us: local(): factor = jnp.linalg.cholesky(gram_matrix + ridge)]
    dot_general x4 -> x0, matrix products: 15.9 us -> none  [the longest x1 4.92 us: local(): pulled = jnp.dot(transforms, errors, precision=highest)]
    another operation x18 -> x0, local copies, waits for them, and re-layouts: 9.37 us -> none
    reshape x2 -> x0, local copies, waits for them, and re-layouts: 8.15 us -> none  [the longest x1 6.02 us: local(): frame_rows = animated.reshape(-1, local_verts)]
    unnamed x17 -> x1, local copies, waits for them, and re-layouts: 6.59 us -> 1.87 us
  transfers between devices with their start and end apart: 2 -> 0, of which waited for: 1 -> 0; matrix products, arithmetic and copies ran while one was open for 0% -> 0% of each run, Pallas kernels for 0% -> 0%
where the time goes in v2:
time: 90.5 us; the launch traced here: 90.3 us
  Pallas kernels  86.1 us (95%)
  between operations  2.34 us (3%)
  local copies, waits for them, and re-layouts  1.87 us (2%)
    pallas_call x1, Pallas kernels, local(): pl.pallas_call(functools.partial(kernel, ridge_scale * verts_total, 1.0 /...  86.1 us
    unnamed x1, local copies, waits for them, and re-layouts  1.87 us

profile of v2, /device:TPU:1, one launch (start us, length us, event | category | flops | bytes accessed | tf_op | source)
XLA Modules:
  0.0 90.3 jit_solution(3284619941782768595)
XLA Ops:
  0.6 86.1 %skinning.1 = (f32[8,8,2048]{2,1,0:T(8,128)}, f32[1,1]{1,0:T(1,128)}) custom-call(f32[384,2048]{1,0:T(8,128)} %bitcast.6, f32[3,2048]{1,0:T(4,128)} %refs_1_.1, s32[1,2048]{1,0:T(1,128)} %bitcast.8, f32[64,2048]{1,0:T(8,128)} %refs_3_.1), custom_call_target="tpu_custom_call" | custom-call | tf_op jit(solution)/shard_map/skinning/pallas_call | solution.py:370
  86.7 1.9 %copy.8 = f32[64,2048]{1,0:T(8,128)} copy(f32[64,2048]{1,0:T(8,128)} %bitcast.7) | data formatting | bytes 1048576

commit v3 on v2

--- a/solution.py
+++ b/solution.py
@@ -21,6 +21,16 @@
 
 def hdot(a, b, dims=NN):
     return lax.dot_general(a, b, dims, precision=HI, preferred_element_type=jnp.float32)
+
+
+def halves(a):
+    high = a.astype(jnp.bfloat16)
+    return high, (a - high.astype(jnp.float32)).astype(jnp.bfloat16)
+
+
+def dot3(a, b):
+    dot = lambda x, y: lax.dot_general(x, y, NN, preferred_element_type=jnp.float32)
+    return dot(a[0], b[0]) + (dot(a[0], b[1]) + dot(a[1], b[0]))
 
 
 def sym(f, n):
@@ -56,12 +66,14 @@
     return [top[i] + off[i] for i in rng] + [[off[j][i] for j in rng] + s[i] for i in rng]
 
 
-def sweep(p, b):
+def sweep(p, b, halfway):
     n = p.shape[0]
     sub = lax.broadcasted_iota(jnp.int32, (n, n), 0)
     lane = lax.broadcasted_iota(jnp.int32, (n, n), 1)
     lane1 = lane[0:1]
     for k in range(0, n, b):
+        if k == n // 2:
+            halfway()
         c = [jnp.broadcast_to(p[:, k + j : k + j + 1], (n, n)) for j in range(b)]
         m = inv_sym(sym(lambda i, j: c[j][k + i : k + i + 1], b))
         r = [
@@ -86,7 +98,7 @@
     for i in range(n // nb):
         s = i * nb
         rows = a[s : s + nb]
-        neg = sweep(rows[:, s : s + nb], b)
+        neg = sweep(rows[:, s : s + nb], b, lambda: between(2 * i))
         w = -hdot(neg, rows)
 
         def parts(middle, full):
@@ -95,7 +107,7 @@
             return jnp.concatenate(left + [middle] + right, axis=1)
 
         a = jnp.where((sub == i) | (lane == i), 0.0, a) - hdot(parts(-eye, rows), parts(neg, w), TN)
-        between(i)
+        between(2 * i + 1)
     return a
 
 
@@ -124,10 +136,11 @@
 
 def reduce_steps(pos, d, bufs, sems, sent):
     b0, acc, b1, sub, b2, gat, full = bufs
+    whole_y = gat is None
     (s0, r0), (s1, r1), (s2, r2), (s3, r3), (s4, r4), (s5, r5) = sems
     half = d.shape[0] // 2
     q = half // NX
-    e = gat.shape[0] // NY
+    e = b2.shape[1]
     xs, ys, core = pos.xs, pos.ys, pos.core
     order = (2, 1, 3, 0)
     c0 = [
@@ -149,29 +162,39 @@
         c1[k].wait_recv()
         tot = tot + b1[k - 1]
     sub[0:q] = tot
-    if NY * e > q:
+    if not whole_y and NY * e > q:
         sub[q:] = jnp.zeros((NY * e - q, 8, 128), jnp.float32)
+    if whole_y:
+        b2[pos.y] = tot
     c2 = {
-        k: send(sub.at[pl.ds(ys[k] * e, e)], b2.at[k - 1], s2.at[k - 1], r2.at[k - 1], pos.yp[k])
+        k: send(
+            sub if whole_y else sub.at[pl.ds(ys[k] * e, e)], b2.at[pos.y if whole_y else k - 1],
+            s2.at[k - 1], r2.at[k - 1], pos.yp[k],
+        )
         for k in far_first
     }
     sent += c2.values()
     yield
-    mine = pl.ds(pos.y * e, e)
-    tot = sub[mine]
     for k in far_first[::-1]:
         c2[k].wait_recv()
-        tot = tot + b2[k - 1]
-    gat[mine] = tot
-    c3 = {
-        k: send(gat.at[mine], gat.at[mine], s3.at[k - 1], r3.at[k - 1], pos.yp[k]) for k in far_first
-    }
-    sent += c3.values()
-    yield
-    for k in far_first[::-1]:
-        c3[k].wait_recv()
+    tot = b2[0]
+    for k in range(1, b2.shape[0]):
+        tot = tot + b2[k]
+    if not whole_y:
+        mine = pl.ds(pos.y * e, e)
+        tot = tot + sub[mine]
+        gat[mine] = tot
+        c3 = {
+            k: send(gat.at[mine], gat.at[mine], s3.at[k - 1], r3.at[k - 1], pos.yp[k])
+            for k in far_first
+        }
+        sent += c3.values()
+        yield
+        for k in far_first[::-1]:
+            c3[k].wait_recv()
+        tot = gat[0:q]
     mine = pl.ds(core * half + pos.x * q, q)
-    full[mine] = gat[0:q]
+    full[mine] = tot
     c4 = {k: send(full.at[mine], full.at[mine], s4.at[k - 1], r4.at[k - 1], pos.xp[k]) for k in (2, 1, 3)}
     c5 = [send(full.at[mine], full.at[mine], s5.at[0], r5.at[0], pos.sib)]
     sent += c4.values()
@@ -191,9 +214,10 @@
     it = iter(refs)
     take = lambda n: [next(it) for _ in range(n)]
     anim, rest_h, lab_h, prior_h, out, f_out = take(6)
-    rows, feats, rest, lab, w_ref, dg, dr, g, gb = take(9)
+    rows, feats, f_high, f_low, rest, lab, w_ref, dg, dr, g, gb = take(11)
     ez, ey, ex, ec, et = take(5)
-    g_bufs, r_bufs = take(7), take(7)
+    g_bufs, r_bufs = take(6), take(7)
+    g_bufs.insert(5, None)
     in_sem, row_sem = take(2)
     pairs = lambda n: [tuple(take(2)) for _ in range(n)]
     g_sems, r_sems = pairs(6), pairs(6)
@@ -230,12 +254,16 @@
         w_ref[:, s] = w
         f = jnp.concatenate([w * rest[k : k + 1, s] for k in range(3)] + [w], axis=0)
         feats[:, s] = f
+        f_high[:, s], f_low[:, s] = halves(f)
         return gram + hdot(f, f, NT)
 
     gram = lax.fori_loop(0, CHUNKS, gram_chunk, jnp.zeros((joint, joint), jnp.float32))
-    gt, rt = joint // 8, n_rows // 8
-    for h in range(2):
-        dg[h * gt : (h + 1) * gt] = gram[:, h * 128 : (h + 1) * 128].reshape(gt, 8, 128)
+    rt = n_rows // 8
+    bt = bones // 8
+    last = jnp.concatenate([gram[bones : 2 * bones, bones : 2 * bones], gram[3 * bones :, 3 * bones :]], axis=1)
+    packed = [gram[:bones, :128], gram[:bones, 128:], gram[bones : 2 * bones, 128:], gram[2 * bones : 3 * bones, 128:], last]
+    for i, part in enumerate(packed):
+        dg[i * bt : (i + 1) * bt] = part.reshape(bt, 8, 128)
     sent = []
     pl.semaphore_wait(barrier, len(peers))
     gsteps = reduce_steps(pos, dg, g_bufs, g_sems, sent)
@@ -254,28 +282,36 @@
     next(rsteps)
     next(gsteps)
     next(rsteps)
-    next(gsteps)
     next(rsteps)
     next(gsteps)
+    next(gsteps)
+    next(gsteps)
     next(rsteps)
-    next(gsteps)
-    next(gsteps)
 
     square = (joint, joint)
     eye = lax.broadcasted_iota(jnp.int32, square, 0) == lax.broadcasted_iota(jnp.int32, square, 1)
     dg, dr = g_bufs[-1], r_bufs[-1]
-    gram = jnp.concatenate([dg[h * gt : (h + 1) * gt].reshape(joint, 128) for h in range(2)], axis=1)
+    p = [dg[i * bt : (i + 1) * bt].reshape(bones, 128) for i in range(5)]
+    blocks = {}
+    pairs_of = (((0, 0), (0, 1)), ((0, 2), (0, 3)), ((1, 2), (1, 3)), ((2, 2), (2, 3)), ((1, 1), (3, 3)))
+    for part, names in zip(p, pairs_of):
+        for i, (k, l) in enumerate(names):
+            blocks[k, l] = blocks[l, k] = part[:, i * bones : (i + 1) * bones]
+    gram = jnp.concatenate(
+        [jnp.concatenate([blocks[k, l] for l in range(4)], axis=1) for k in range(4)], axis=0
+    )
     gram = gram + jnp.where(eye, ridge, 0.0)
-    neg = negative_inverse(gram, 64, 4, lambda i: next(rsteps) if i < 3 else None)
+    neg = negative_inverse(gram, 64, 4, lambda i: next(rsteps) if i in (4, 6, 7) else None)
     rhs = jnp.concatenate([dr[h * rt : (h + 1) * rt].reshape(n_rows, 128) for h in range(2)], axis=1)
     tt = -hdot(rhs, neg)
-    tt = tt - hdot(rhs - hdot(tt, gram), neg)
-    t = tt.T
+    left = (rhs - hdot(tt, gram)).astype(jnp.bfloat16)
+    tt = tt - jnp.dot(left, neg.astype(jnp.bfloat16), preferred_element_type=jnp.float32)
+    tt_parts, t_parts = halves(tt), halves(tt.T)
 
     def fit_chunk(j, squares):
         s = pl.ds(pl.multiple_of(j * cv, cv), cv)
-        e = rows[:, s] - hdot(tt, feats[:, s])
-        pulled = hdot(t, e)
+        e = rows[:, s] - dot3(tt_parts, (f_high[:, s], f_low[:, s]))
+        pulled = dot3(t_parts, halves(e))
         grad = pulled[3 * bones :]
         for k in range(3):
             grad = grad + pulled[k * bones : (k + 1) * bones] * rest[k : k + 1, s]
@@ -286,7 +322,7 @@
         return squares + total([sq[:, i * 128 : (i + 1) * 128] for i in range(cv // 128)])
 
     et[0] = lax.fori_loop(0, CHUNKS, fit_chunk, jnp.zeros((8, 128), jnp.float32))
-    cz = [send(et.at[0], ez.at[k - 1], sz.at[k - 1], rz.at[k - 1], pos.zp[k]) for k in far_first]
+    cz = [send(et.at[0], ez.at[pos.z], sz.at[k - 1], rz.at[k - 1], pos.zp[k]) for k in far_first]
 
     mine = pl.ds(pl.multiple_of(pos.z * (bones // NZ), bones // NZ), bones // NZ)
 
@@ -306,21 +342,23 @@
 
     lax.fori_loop(0, CHUNKS, update_chunk, 0)
 
-    def add_up(copies, buf, i):
-        tot = et[i]
+    def add_up(copies, buf, at, i):
+        buf[at] = et[i]
         for cp in copies:
             cp.wait_recv()
-        for k in range(buf.shape[0]):
+        tot = buf[0]
+        for k in range(1, buf.shape[0]):
             tot = tot + buf[k]
         et[i + 1] = tot
 
-    add_up(cz, ez, 0)
-    cy = [send(et.at[1], ey.at[k - 1], sy.at[k - 1], ry.at[k - 1], pos.yp[k]) for k in far_first]
-    add_up(cy, ey, 1)
-    cx = [send(et.at[2], ex.at[k - 1], sx.at[k - 1], rx.at[k - 1], pos.xp[k]) for k in (2, 1, 3)]
-    add_up(cx, ex, 2)
+    add_up(cz, ez, pos.z, 0)
+    cy = [send(et.at[1], ey.at[pos.y], sy.at[k - 1], ry.at[k - 1], pos.yp[k]) for k in far_first]
+    add_up(cy, ey, pos.y, 1)
+    cx = [send(et.at[2], ex.at[pos.x], sx.at[k - 1], rx.at[k - 1], pos.xp[k]) for k in (2, 1, 3)]
+    add_up(cx, ex, pos.x, 2)
     cc = [send(et.at[3], ec.at[0], sc.at[0], rc.at[0], pos.sib)]
-    add_up(cc, ec, 3)
+    cc[0].wait_recv()
+    et[4] = et[3] + ec[0]
     f_out[...] = jnp.sum(et[4], axis=(0, 1), keepdims=True) * scale
 
     def gather_chunk(j, carry):
@@ -348,20 +386,24 @@
     vmem = lambda *s: pltpu.VMEM(s, jnp.float32)
     tiles = lambda *s: vmem(*s, 8, 128)
 
-    def buffers(n):
+    def buffers(n, whole_y):
         q = n // (2 * NX)
         e = -(-q // NY)
-        return [tiles(NX, q), tiles(NX, q), tiles(NX - 1, q), tiles(NY * e), tiles(NY - 1, e), tiles(NY * e), tiles(n)]
+        common = [tiles(NX, q), tiles(NX, q), tiles(NX - 1, q)]
+        if whole_y:
+            return common + [tiles(q), tiles(NY, q), tiles(n)]
+        return common + [tiles(NY * e), tiles(NY - 1, e), tiles(NY * e), tiles(n)]
 
     pair = lambda *s: [pltpu.SemaphoreType.DMA(s)] * 2
     reduce_pairs = pair(4) + pair(3) + pair(7) + pair(7) + pair(3) + pair(4)
-    n_gram, n_rhs = joint * joint // 1024, n_rows * joint // 1024
+    n_gram, n_rhs = 10 * bones * bones // 1024, n_rows * joint // 1024
     scratch = [
-        vmem(n_rows, verts), vmem(joint, verts), vmem(3, verts), pltpu.VMEM((1, verts), jnp.int32),
+        vmem(n_rows, verts), vmem(joint, verts),
+        pltpu.VMEM((joint, verts), jnp.bfloat16), pltpu.VMEM((joint, verts), jnp.bfloat16), vmem(3, verts), pltpu.VMEM((1, verts), jnp.int32),
         vmem(bones, verts), tiles(n_gram), tiles(n_rhs), vmem(NZ, bones // NZ, verts),
-        vmem(NZ - 1, bones // NZ, verts), tiles(NZ - 1), tiles(NY - 1), tiles(NX - 1), tiles(1), tiles(5),
+        vmem(NZ - 1, bones // NZ, verts), tiles(NZ), tiles(NY), tiles(NX), tiles(1), tiles(5),
     ]
-    scratch += buffers(n_gram) + buffers(n_rhs)
+    scratch += buffers(n_gram, True) + buffers(n_rhs, False)
     scratch += [pltpu.SemaphoreType.DMA((3,)), pltpu.SemaphoreType.DMA((CHUNKS,))]
     scratch += reduce_pairs + reduce_pairs
     scratch += pair(CHUNKS, NZ - 1) + pair(CHUNKS, NZ - 1) + pair(NZ - 1) + pair(NY - 1) + pair(NX - 1) + pair(1)

time: 90.5 us -> 86.8 us (0.959)
  Pallas kernels: 86.1 us -> 82.4 us
    pallas_call x1, Pallas kernels: 86.1 us -> 82.4 us  [local(): pl.pallas_call(functools.partial(kernel, ridge_scale * verts_total, 1.0 /...]
where the time goes in v3:
time: 86.8 us; the launch traced here: 86.6 us
  Pallas kernels  82.4 us (95%)
  between operations  2.34 us (3%)
  local copies, waits for them, and re-layouts  1.87 us (2%)
    pallas_call x1, Pallas kernels, local(): pl.pallas_call(functools.partial(kernel, ridge_scale * verts_total, 1.0 /...  82.4 us
    unnamed x1, local copies, waits for them, and re-layouts  1.87 us

profile of v3, /device:TPU:1, one launch (start us, length us, event | category | flops | bytes accessed | tf_op | source)
XLA Modules:
  0.0 86.6 jit_solution(4645594085126356343)
XLA Ops:
  0.6 82.4 %skinning.1 = (f32[8,8,2048]{2,1,0:T(8,128)}, f32[1,1]{1,0:T(1,128)}) custom-call(f32[384,2048]{1,0:T(8,128)} %bitcast.6, f32[3,2048]{1,0:T(4,128)} %refs_1_.1, s32[1,2048]{1,0:T(1,128)} %bitcast.8, f32[64,2048]{1,0:T(8,128)} %refs_3_.1), custom_call_target="tpu_custom_call" | custom-call | tf_op jit(solution)/shard_map/skinning/pallas_call | solution.py:412
  83.0 1.9 %copy.8 = f32[64,2048]{1,0:T(8,128)} copy(f32[64,2048]{1,0:T(8,128)} %bitcast.7) | data formatting | bytes 1048576

commit v4 on v3

--- a/solution.py
+++ b/solution.py
@@ -99,6 +99,8 @@
         s = i * nb
         rows = a[s : s + nb]
         neg = sweep(rows[:, s : s + nb], b, lambda: between(2 * i))
+        if i == n // nb - 1:
+            between(2 * i + 1)
         w = -hdot(neg, rows)
 
         def parts(middle, full):
@@ -107,7 +109,7 @@
             return jnp.concatenate(left + [middle] + right, axis=1)
 
         a = jnp.where((sub == i) | (lane == i), 0.0, a) - hdot(parts(-eye, rows), parts(neg, w), TN)
-        between(2 * i + 1)
+        between(2 * i + 1 + i // (n // nb - 1))
     return a
 
 
@@ -214,7 +216,7 @@
     it = iter(refs)
     take = lambda n: [next(it) for _ in range(n)]
     anim, rest_h, lab_h, prior_h, out, f_out = take(6)
-    rows, feats, f_high, f_low, rest, lab, w_ref, dg, dr, g, gb = take(11)
+    rows, feats, rest, lab, w_ref, dg, dr, g, gb = take(9)
     ez, ey, ex, ec, et = take(5)
     g_bufs, r_bufs = take(6), take(7)
     g_bufs.insert(5, None)
@@ -254,7 +256,6 @@
         w_ref[:, s] = w
         f = jnp.concatenate([w * rest[k : k + 1, s] for k in range(3)] + [w], axis=0)
         feats[:, s] = f
-        f_high[:, s], f_low[:, s] = halves(f)
         return gram + hdot(f, f, NT)
 
     gram = lax.fori_loop(0, CHUNKS, gram_chunk, jnp.zeros((joint, joint), jnp.float32))
@@ -301,16 +302,16 @@
         [jnp.concatenate([blocks[k, l] for l in range(4)], axis=1) for k in range(4)], axis=0
     )
     gram = gram + jnp.where(eye, ridge, 0.0)
-    neg = negative_inverse(gram, 64, 4, lambda i: next(rsteps) if i in (4, 6, 7) else None)
+    neg = negative_inverse(gram, 64, 4, lambda i: next(rsteps) if i in (3, 7, 8) else None)
     rhs = jnp.concatenate([dr[h * rt : (h + 1) * rt].reshape(n_rows, 128) for h in range(2)], axis=1)
-    tt = -hdot(rhs, neg)
-    left = (rhs - hdot(tt, gram)).astype(jnp.bfloat16)
-    tt = tt - jnp.dot(left, neg.astype(jnp.bfloat16), preferred_element_type=jnp.float32)
-    tt_parts, t_parts = halves(tt), halves(tt.T)
+    neg_parts = halves(neg)
+    tt = -dot3(halves(rhs), neg_parts)
+    tt = tt - dot3(halves(rhs - hdot(tt, gram)), neg_parts)
+    t_parts = halves(tt.T)
 
     def fit_chunk(j, squares):
         s = pl.ds(pl.multiple_of(j * cv, cv), cv)
-        e = rows[:, s] - dot3(tt_parts, (f_high[:, s], f_low[:, s]))
+        e = rows[:, s] - hdot(tt, feats[:, s])
         pulled = dot3(t_parts, halves(e))
         grad = pulled[3 * bones :]
         for k in range(3):
@@ -399,7 +400,7 @@
     n_gram, n_rhs = 10 * bones * bones // 1024, n_rows * joint // 1024
     scratch = [
         vmem(n_rows, verts), vmem(joint, verts),
-        pltpu.VMEM((joint, verts), jnp.bfloat16), pltpu.VMEM((joint, verts), jnp.bfloat16), vmem(3, verts), pltpu.VMEM((1, verts), jnp.int32),
+        vmem(3, verts), pltpu.VMEM((1, verts), jnp.int32),
         vmem(bones, verts), tiles(n_gram), tiles(n_rhs), vmem(NZ, bones // NZ, verts),
         vmem(NZ - 1, bones // NZ, verts), tiles(NZ), tiles(NY), tiles(NX), tiles(1), tiles(5),
     ]
@@ -419,10 +420,10 @@
         out_specs=(vm, vm),
         scratch_shapes=scratch,
         compiler_params=pltpu.CompilerParams(
-            collective_id=0, has_side_effects=True, vmem_limit_bytes=56 << 20
+            collective_id=0, has_side_effects=True, vmem_limit_bytes=28 << 20
         ),
         name="skinning",
-    )(rows, rest_positions, labels.reshape(1, verts), weight_prior)
+    )(*[pltpu.with_memory_space_constraint(a, pltpu.HBM) for a in (rows, rest_positions, labels.reshape(1, verts), weight_prior)])
     return new_weights.reshape(bones, verts), fit_error.reshape(())
 
 

time: 86.8 us -> 85.7 us (0.987)
  local copies, waits for them, and re-layouts: 1.87 us -> 0.8 us
    unnamed x1, local copies, waits for them, and re-layouts: 1.87 us -> 0.8 us
where the time goes in v4:
time: 85.7 us; the launch traced here: 85.5 us
  Pallas kernels  82.3 us (96%)
  between operations  2.33 us (3%)
    pallas_call x1, Pallas kernels, local(): pl.pallas_call(functools.partial(kernel, ridge_scale * verts_total, 1.0 /...  82.3 us

profile of v4, /device:TPU:1, one launch (start us, length us, event | category | flops | bytes accessed | tf_op | source)
XLA Modules:
  0.0 85.5 jit_solution(12401308018122398032)
XLA Ops:
  0.6 82.3 %skinning.1 = (f32[8,8,2048]{2,1,0:T(8,128)S(1)}, f32[1,1]{1,0:T(1,128)}) custom-call(f32[384,2048]{1,0:T(8,128)} %bitcast.7, f32[3,2048]{1,0:T(4,128)} %refs_1_.1, s32[1,2048]{1,0:T(1,128)} %bitcast.8, f32[64,2048]{1,0:T(8,128)} %refs_3_.1), custom_call_target="tpu_custom_call" | custom-call | tf_op jit(solution)/shard_map/skinning/pallas_call | solution.py:413
  83.0 0.8 copy.8

commit v5 on v4

--- a/solution.py
+++ b/solution.py
@@ -66,14 +66,14 @@
     return [top[i] + off[i] for i in rng] + [[off[j][i] for j in rng] + s[i] for i in rng]
 
 
-def sweep(p, b, halfway):
+def sweep(p, b, late):
     n = p.shape[0]
     sub = lax.broadcasted_iota(jnp.int32, (n, n), 0)
     lane = lax.broadcasted_iota(jnp.int32, (n, n), 1)
     lane1 = lane[0:1]
     for k in range(0, n, b):
-        if k == n // 2:
-            halfway()
+        if k == 3 * n // 4:
+            late()
         c = [jnp.broadcast_to(p[:, k + j : k + j + 1], (n, n)) for j in range(b)]
         m = inv_sym(sym(lambda i, j: c[j][k + i : k + i + 1], b))
         r = [
@@ -231,6 +231,10 @@
     cv = verts // CHUNKS
     pos = Place()
 
+    barrier = pltpu.get_barrier_semaphore()
+    peers = [pos.sib] + pos.xp[1:] + pos.yp[1:] + pos.zp[1:]
+    for p in peers:
+        pl.semaphore_signal(barrier, inc=1, device_id=p, device_id_type=MESH)
     small = [
         pltpu.make_async_copy(src, dst, in_sem.at[i])
         for i, (src, dst) in enumerate(((prior_h, w_ref), (rest_h, rest), (lab_h, lab)))
@@ -240,10 +244,6 @@
     for j in range(CHUNKS):
         s = pl.ds(j * cv, cv)
         pltpu.make_async_copy(anim.at[:, s], rows.at[:, s], row_sem.at[j]).start()
-    barrier = pltpu.get_barrier_semaphore()
-    peers = [pos.sib] + pos.xp[1:] + pos.yp[1:] + pos.zp[1:]
-    for p in peers:
-        pl.semaphore_signal(barrier, inc=1, device_id=p, device_id_type=MESH)
     for cp in small:
         cp.wait()
 
@@ -276,18 +276,19 @@
         pltpu.make_async_copy(anim.at[:, s], rows.at[:, s], row_sem.at[j]).wait()
         return rhs + hdot(rows[:, s], feats[:, s], NT)
 
-    next(gsteps)
-    rhs = lax.fori_loop(0, CHUNKS, rhs_chunk, jnp.zeros((n_rows, joint), jnp.float32))
+    rhs = lax.fori_loop(0, 1, rhs_chunk, jnp.zeros((n_rows, joint), jnp.float32))
+    next(gsteps)
+    rhs = lax.fori_loop(1, CHUNKS, rhs_chunk, rhs)
     for h in range(2):
         dr[h * rt : (h + 1) * rt] = rhs[:, h * 128 : (h + 1) * 128].reshape(rt, 8, 128)
     next(rsteps)
-    next(gsteps)
     next(rsteps)
+    next(gsteps)
     next(rsteps)
     next(gsteps)
-    next(gsteps)
-    next(gsteps)
     next(rsteps)
+    next(gsteps)
+    next(gsteps)
 
     square = (joint, joint)
     eye = lax.broadcasted_iota(jnp.int32, square, 0) == lax.broadcasted_iota(jnp.int32, square, 1)
@@ -302,7 +303,7 @@
         [jnp.concatenate([blocks[k, l] for l in range(4)], axis=1) for k in range(4)], axis=0
     )
     gram = gram + jnp.where(eye, ridge, 0.0)
-    neg = negative_inverse(gram, 64, 4, lambda i: next(rsteps) if i in (3, 7, 8) else None)
+    neg = negative_inverse(gram, 64, 4, lambda i: next(rsteps) if i in (2, 7, 8) else None)
     rhs = jnp.concatenate([dr[h * rt : (h + 1) * rt].reshape(n_rows, 128) for h in range(2)], axis=1)
     neg_parts = halves(neg)
     tt = -dot3(halves(rhs), neg_parts)

time: 85.7 us -> 85 us (level)
  Pallas kernels: 82.3 us -> 81.4 us
    pallas_call x1, Pallas kernels: 82.3 us -> 81.4 us  [local(): pl.pallas_call(functools.partial(kernel, ridge_scale * verts_total, 1.0 /...]
where the time goes in v5:
time: 85 us; the launch traced here: 84.5 us
  Pallas kernels  81.4 us (96%)
  between operations  2.33 us (3%)
    pallas_call x1, Pallas kernels, local(): pl.pallas_call(functools.partial(kernel, ridge_scale * verts_total, 1.0 /...  81.4 us

profile of v5, /device:TPU:1, one launch (start us, length us, event | category | flops | bytes accessed | tf_op | source)
XLA Modules:
  0.0 84.5 jit_solution(9886401253021445245)
XLA Ops:
  0.6 81.4 %skinning.1 = (f32[8,8,2048]{2,1,0:T(8,128)S(1)}, f32[1,1]{1,0:T(1,128)}) custom-call(f32[384,2048]{1,0:T(8,128)} %bitcast.7, f32[3,2048]{1,0:T(4,128)} %refs_1_.1, s32[1,2048]{1,0:T(1,128)} %bitcast.8, f32[64,2048]{1,0:T(8,128)} %refs_3_.1), custom_call_target="tpu_custom_call" | custom-call | tf_op jit(solution)/shard_map/skinning/pallas_call | solution.py:414
  82.0 0.8 copy.8

commit v6 on v5

--- a/solution.py
+++ b/solution.py
@@ -372,9 +372,9 @@
             ).wait()
         return carry
 
-    lax.fori_loop(0, CHUNKS, gather_chunk, 0)
     for cp in sent + cz + cy + cx + cc:
         cp.wait_send()
+    lax.fori_loop(0, CHUNKS, gather_chunk, 0)
 
 
 def local(animated, rest_positions, labels, weight_prior):

time: 85 us -> 84.9 us (level)
  no operation moved by 1% of the time
where the time goes in v6:
time: 84.9 us; the launch traced here: 84.5 us
  Pallas kernels  81.4 us (96%)
  between operations  2.33 us (3%)
    pallas_call x1, Pallas kernels, local(): pl.pallas_call(functools.partial(kernel, ridge_scale * verts_total, 1.0 /...  81.4 us

profile of v6, /device:TPU:1, one launch (start us, length us, event | category | flops | bytes accessed | tf_op | source)
XLA Modules:
  0.0 84.5 jit_solution(9234108111720222962)
XLA Ops:
  0.6 81.4 %skinning.1 = (f32[8,8,2048]{2,1,0:T(8,128)S(1)}, f32[1,1]{1,0:T(1,128)}) custom-call(f32[384,2048]{1,0:T(8,128)} %bitcast.7, f32[3,2048]{1,0:T(4,128)} %refs_1_.1, s32[1,2048]{1,0:T(1,128)} %bitcast.8, f32[64,2048]{1,0:T(8,128)} %refs_3_.1), custom_call_target="tpu_custom_call" | custom-call | tf_op jit(solution)/shard_map/skinning/pallas_call | solution.py:414
  82.0 0.8 copy.8
